TPU v7x, 128 devices: a whole 4x4x4 slice. The times are simulated.
128 devices in a mesh: row: 16 (over x, z_hi, core), col: 8 (over z_lo, y).
Axes of the slice: x: 4, y: 4, z: 4 (z_hi: 2, z_lo: 2; z = z_hi * 2 + z_lo), core: 2. Of those that a mesh axis runs over, the one named last changes fastest.
Arguments:
- pair: bfloat16 [1024, 1024, 128], P('row', 'col'), may hold values from -6 to 6
- bias_weight: bfloat16 [128, 16], replicated
- single: bfloat16 [48, 1024, 768], P('col', 'row'), may hold values from -6 to 6
- w_qkv: bfloat16 [768, 2304], replicated, may hold values from -0.21875 to 0.21875
- w_out: bfloat16 [768, 768], replicated, may hold values from -0.21875 to 0.21875
- w_gate_up: bfloat16 [768, 3072], replicated, may hold values from -0.21875 to 0.21875
- w_down: bfloat16 [1536, 768], replicated, may hold values from -0.15625 to 0.15625
- cotangent: bfloat16 [48, 1024, 768], P('col', 'row'), may hold values from -300 to 300
Outputs:
- updated: bfloat16 [48, 1024, 768], P('col', 'row')
- pair_grad: float32 [1024, 1024, 128], P('row', 'col')
All inputs are finite; a program needn't handle non-finite values.
Results may differ from a plain program's by a relative error of at most 0.012.
The roundings to bfloat16 on the way count: a program that leaves them out, or rounds other values in their place, can miss the bound.
Values may be sent and summed in bfloat16 or wider, within the bound.
No kernel may reach another device: no remote copies, remote signals or barrier semaphores. Data moves between devices by JAX's collectives and lax.ppermute only.
A program may use at most 192 MiB of HBM per device.

v0:
```python
import math
import jax
import jax.numpy as jnp
from jax import lax
from jax.sharding import PartitionSpec as P


def normalize(values):
    mean_val = jnp.mean(values, axis=-1, keepdims=True)
    centred = values - mean_val
    variance = jnp.mean(centred * centred, axis=-1, keepdims=True)
    scaled = lax.rsqrt(variance + 1e-05)
    return (centred * scaled, scaled)


def project_pair(piece, bias_weight):
    normed_pair, scaled = normalize(piece.astype(jnp.float32))
    row_count, col_count, chans = normed_pair.shape
    flat = jnp.dot(
        normed_pair.reshape(row_count * col_count, chans),
        bias_weight.astype(jnp.float32),
        precision=lax.Precision.HIGHEST,
    )
    return jnp.transpose(flat.reshape(row_count, col_count, -1), (2, 0, 1)).astype(jnp.bfloat16)


def attend_sample(queries, key_rows, value_rows, cotan, bias, head_count):
    row_count, width = queries.shape
    head_size = width // head_count
    query_h = queries.reshape(row_count, head_count, head_size)
    key_h = key_rows.reshape(-1, head_count, head_size)
    value_h = value_rows.reshape(-1, head_count, head_size)
    cotan_h = cotan.reshape(row_count, head_count, head_size)
    scores = jnp.einsum(
        "ihe,jhe->hij", query_h, key_h, preferred_element_type=jnp.float32
    ) / math.sqrt(head_size) + bias.astype(jnp.float32)
    weights = jax.nn.softmax(scores, axis=-1)
    rounded = weights.astype(jnp.bfloat16)
    attended = jnp.einsum("hij,jhe->ihe", rounded, value_h, preferred_element_type=jnp.float32)
    dprob = jnp.einsum("ihe,jhe->hij", cotan_h, value_h, preferred_element_type=jnp.float32)
    row_delta = jnp.sum(cotan_h.astype(jnp.float32) * attended, axis=2)
    grad_term = weights * (dprob - jnp.transpose(row_delta)[:, :, None])
    return (attended.reshape(row_count, width), grad_term)


def transition(single, attended, w_out, w_gate_up, w_down):
    width = single.shape[-1]
    flat_in = single.reshape(-1, width).astype(jnp.float32)
    mid = flat_in + jnp.dot(
        attended.reshape(-1, width).astype(jnp.bfloat16), w_out, preferred_element_type=jnp.float32
    )
    normed_mid = normalize(mid)[0].astype(jnp.bfloat16)
    gate_up = jnp.dot(normed_mid, w_gate_up, preferred_element_type=jnp.float32)
    half = gate_up.shape[1] // 2
    hidden = (jax.nn.silu(gate_up[:, :half]) * gate_up[:, half:]).astype(jnp.bfloat16)
    result = mid + jnp.dot(hidden, w_down, preferred_element_type=jnp.float32)
    return result.astype(jnp.bfloat16).reshape(single.shape)


def back_norm(normed_grad, normed_pair, scaled):
    centred = normed_grad - jnp.mean(normed_grad, axis=-1, keepdims=True)
    along = jnp.mean(normed_grad * normed_pair, axis=-1, keepdims=True)
    return (centred - normed_pair * along) * scaled


def shards(pair, bias_weight, single, w_qkv, w_out, w_gate_up, w_down, cotangent):
    width = single.shape[2]
    head_count = bias_weight.shape[1]
    samp_count, row_count = (single.shape[0], single.shape[1])
    bias = lax.all_gather(project_pair(pair, bias_weight), "col", axis=2, tiled=True)
    normed = normalize(single.astype(jnp.float32))[0].astype(jnp.bfloat16)
    flat_normed = normed.reshape(samp_count * row_count, width)
    queries = jnp.dot(flat_normed, w_qkv[:, :width], preferred_element_type=jnp.float32).astype(
        jnp.bfloat16
    )
    queries = queries.reshape(samp_count, row_count, width)
    w_kv = w_qkv[:, width:]
    kv_local = jnp.dot(flat_normed, w_kv, preferred_element_type=jnp.float32).astype(jnp.bfloat16)
    kv_local = kv_local.reshape(samp_count, row_count, 2 * width)
    kv_all = lax.all_gather(kv_local, "row", axis=1, tiled=True)

    def one_sample(carry, inputs):
        query_s, kv_s, cotan_s = inputs
        attended, grad_term = attend_sample(
            query_s, kv_s[:, :width], kv_s[:, width:], cotan_s, bias, head_count
        )
        return (carry + grad_term, attended)

    start_grad = jnp.zeros((head_count, row_count, kv_all.shape[1]), jnp.float32)
    grad_local, attended = lax.scan(one_sample, start_grad, (queries, kv_all, cotangent))
    updated = transition(single, attended, w_out, w_gate_up, w_down)
    bias_grad = lax.psum_scatter(grad_local, "col", scatter_dimension=2, tiled=True)
    normed_pair, scaled = normalize(pair.astype(jnp.float32))
    col_count, chans = (pair.shape[1], pair.shape[2])
    flat_grad = jnp.transpose(bias_grad, (1, 2, 0)).reshape(row_count * col_count, head_count)
    normed_grad = jnp.dot(
        flat_grad, jnp.transpose(bias_weight.astype(jnp.float32)), precision=lax.Precision.HIGHEST
    )
    normed_grad = normed_grad.reshape(row_count, col_count, chans)
    pair_grad = back_norm(normed_grad, normed_pair, scaled)
    return (updated, pair_grad)


def solution(mesh):
    return jax.shard_map(
        shards,
        mesh=mesh,
        in_specs=(
            P("row", "col", None),
            P(),
            P("col", "row", None),
            P(),
            P(),
            P(),
            P(),
            P("col", "row", None),
        ),
        out_specs=(P("col", "row", None), P("row", "col", None)),
        check_vma=False,
    )
```

profile of v0, /device:TPU:1, one launch (start us, length us, event | category | flops | bytes accessed | tf_op | source)
XLA Modules:
  0.0 442.7 jit_solution(11677037070908961696)
XLA Ops:
  7.2 4.2 copy.27
  11.5 2.2 convert_reduce_fusion
  13.7 0.8 fusion.18
  14.6 2.5 fusion.29
  17.9 4.0 convolution_convert_fusion
  22.0 2.9 convolution_convert_fusion.1
  24.9 36.6 %all-gather.5.cloned.1.call-done = bf16[16,64,1024]{2,0,1:T(8,128)(2,1)} async-done(((bf16[16,64,128]{2,0,1:T(8,128)(2,1)}), bf16[16,64,1024]{2,0,1:T(8,128)(2,1)}) %all-gather.5.cloned.1.call-update) | async-done | bytes 2097168 | tf_op jit(solution)/shard_map/all_gather | solution.py:70
  61.5 4.0 copy.31
  65.5 124.4 %all-gather.3.cloned.1.call-done = bf16[6,1024,1536]{2,1,0:T(8,128)(2,1)} async-done(((bf16[6,64,1536]{2,1,0:T(8,128)(2,1)}), bf16[6,1024,1536]{2,1,0:T(8,128)(2,1)}) %all-gather.3.cloned.1.call-update) | async-done | bytes 18874384 | tf_op jit(solution)/shard_map/all_gather | solution.py:80
  190.0 182.2 %while.13 = (s32[]{:T(128)}, f32[16,64,1024]{2,1,0:T(8,128)}, bf16[6,64,768]{2,1,0:T(8,128)(2,1)}, bf16[6,64,768]{2,1,0:T(8,128)(2,1)}, bf16[6,1024,1536]{2,1,0:...) while((s32[]{:T(128)}, f32[16,64,1024]{2,1,0:T(8,128)}, ...), condition=%wide.region_8.9_spmd.clone, body=%wide.region_4.8_spmd.clone.sunk | while | flops 314769408 | bytes 48255596 | solution.py:90
  190.0 1.0 constant_dynamic-slice_fusion.5
  191.1 3.8 constant_dynamic-slice_fusion.6
  194.9 4.7 %copy.59 = bf16[1,1024,1536]{1,2,0:T(8,128)(2,1)} copy(bf16[1,1024,1536]{2,1,0:T(8,128)(2,1)} %constant_dynamic-slice_fusion.6) | data formatting | bytes 6291456 | tf_op jit(solution)/shard_map/while/body/jit(dynamic_index_in_dim)/dynamic_slice | solution.py:90
  199.5 3.9 fusion.68
  203.4 5.7 %fusion.69 = (f32[16,64]{1,0:T(8,128)S(1)}, f32[16,64,1024]{2,1,0:T(8,128)}) fusion(bf16[16,64,1024]{2,1,0:T(8,128)(2,1)} %get-tuple-element.206, bf16[64,16,48]{0,2,1:T(8,128)(2,1)S(1)} %bitcast.70, bf16[1024,16,48]{0,2,1:T(8,128)(2,1)} %bitcast.67), kind=kOutput, calls=%fused_computation.64.clone.1 | convolution fusion | flops 105907200 | bytes 7966720 | tf_op jit(solution)/shard_map/while/body/eval_jaxpr/sub | solution.py:37
  209.3 3.5 fusion.70
  212.8 5.8 %select_add_fusion.2 = f32[16,64,1024]{2,1,0:T(8,128)} fusion(f32[16,64,1024]{2,1,0:T(8,128)} %get-tuple-element.193, bf16[64,16,48]{0,2,1:T(8,128)(2,1)S(1)} %bitcast.73, bf16[1024,16,48]{0,2,1:T(8,128)(2,1)} %bitcast.69, f32[16,64]{1,0:T(8,128)S(1)} %bitcast.82, pred[]{:T(512)S(6)} %compare.3, f32[16,64,1024]{2,1,0:T(8,128)} %get-tuple-element.179, ...), kind=kOutput, calls=%fused_computation.1.clone.1 | convolution fusion | flops 105906176 | bytes 14262273 | tf_op jit(solution)/shard_map/while/body/eval_jaxpr/ihe,jhe->hij/dot_general | solution.py:40
  218.7 0.7 constant_dynamic-update-slice_fusion.2
  219.3 1.0 constant_dynamic-slice_fusion.5
  220.4 3.8 constant_dynamic-slice_fusion.6
  224.2 4.7 %copy.59 = bf16[1,1024,1536]{1,2,0:T(8,128)(2,1)} copy(bf16[1,1024,1536]{2,1,0:T(8,128)(2,1)} %constant_dynamic-slice_fusion.6) | data formatting | bytes 6291456 | tf_op jit(solution)/shard_map/while/body/jit(dynamic_index_in_dim)/dynamic_slice | solution.py:90
  228.9 3.9 fusion.68
  232.8 5.7 %fusion.69 = (f32[16,64]{1,0:T(8,128)S(1)}, f32[16,64,1024]{2,1,0:T(8,128)}) fusion(bf16[16,64,1024]{2,1,0:T(8,128)(2,1)} %get-tuple-element.206, bf16[64,16,48]{0,2,1:T(8,128)(2,1)S(1)} %bitcast.70, bf16[1024,16,48]{0,2,1:T(8,128)(2,1)} %bitcast.67), kind=kOutput, calls=%fused_computation.64.clone.1 | convolution fusion | flops 105907200 | bytes 7966720 | tf_op jit(solution)/shard_map/while/body/eval_jaxpr/sub | solution.py:37
  238.6 3.5 fusion.70
  242.1 7.0 %select_add_fusion.2 = f32[16,64,1024]{2,1,0:T(8,128)} fusion(f32[16,64,1024]{2,1,0:T(8,128)} %get-tuple-element.193, bf16[64,16,48]{0,2,1:T(8,128)(2,1)S(1)} %bitcast.73, bf16[1024,16,48]{0,2,1:T(8,128)(2,1)} %bitcast.69, f32[16,64]{1,0:T(8,128)S(1)} %bitcast.82, pred[]{:T(512)S(6)} %compare.3, f32[16,64,1024]{2,1,0:T(8,128)} %get-tuple-element.179, ...), kind=kOutput, calls=%fused_computation.1.clone.1 | convolution fusion | flops 105906176 | bytes 14262273 | tf_op jit(solution)/shard_map/while/body/eval_jaxpr/ihe,jhe->hij/dot_general | solution.py:40
  249.9 1.0 constant_dynamic-slice_fusion.5
  251.0 3.8 constant_dynamic-slice_fusion.6
  254.8 4.7 %copy.59 = bf16[1,1024,1536]{1,2,0:T(8,128)(2,1)} copy(bf16[1,1024,1536]{2,1,0:T(8,128)(2,1)} %constant_dynamic-slice_fusion.6) | data formatting | bytes 6291456 | tf_op jit(solution)/shard_map/while/body/jit(dynamic_index_in_dim)/dynamic_slice | solution.py:90
  259.4 3.9 fusion.68
  263.4 5.7 %fusion.69 = (f32[16,64]{1,0:T(8,128)S(1)}, f32[16,64,1024]{2,1,0:T(8,128)}) fusion(bf16[16,64,1024]{2,1,0:T(8,128)(2,1)} %get-tuple-element.206, bf16[64,16,48]{0,2,1:T(8,128)(2,1)S(1)} %bitcast.70, bf16[1024,16,48]{0,2,1:T(8,128)(2,1)} %bitcast.67), kind=kOutput, calls=%fused_computation.64.clone.1 | convolution fusion | flops 105907200 | bytes 7966720 | tf_op jit(solution)/shard_map/while/body/eval_jaxpr/sub | solution.py:37
  269.2 3.5 fusion.70
  272.7 7.0 %select_add_fusion.2 = f32[16,64,1024]{2,1,0:T(8,128)} fusion(f32[16,64,1024]{2,1,0:T(8,128)} %get-tuple-element.193, bf16[64,16,48]{0,2,1:T(8,128)(2,1)S(1)} %bitcast.73, bf16[1024,16,48]{0,2,1:T(8,128)(2,1)} %bitcast.69, f32[16,64]{1,0:T(8,128)S(1)} %bitcast.82, pred[]{:T(512)S(6)} %compare.3, f32[16,64,1024]{2,1,0:T(8,128)} %get-tuple-element.179, ...), kind=kOutput, calls=%fused_computation.1.clone.1 | convolution fusion | flops 105906176 | bytes 14262273 | tf_op jit(solution)/shard_map/while/body/eval_jaxpr/ihe,jhe->hij/dot_general | solution.py:40
  279.8 0.7 constant_dynamic-update-slice_fusion.2
  280.5 1.0 constant_dynamic-slice_fusion.5
  281.6 3.8 constant_dynamic-slice_fusion.6
  285.3 4.7 %copy.59 = bf16[1,1024,1536]{1,2,0:T(8,128)(2,1)} copy(bf16[1,1024,1536]{2,1,0:T(8,128)(2,1)} %constant_dynamic-slice_fusion.6) | data formatting | bytes 6291456 | tf_op jit(solution)/shard_map/while/body/jit(dynamic_index_in_dim)/dynamic_slice | solution.py:90
  290.0 3.9 fusion.68
  293.9 5.7 %fusion.69 = (f32[16,64]{1,0:T(8,128)S(1)}, f32[16,64,1024]{2,1,0:T(8,128)}) fusion(bf16[16,64,1024]{2,1,0:T(8,128)(2,1)} %get-tuple-element.206, bf16[64,16,48]{0,2,1:T(8,128)(2,1)S(1)} %bitcast.70, bf16[1024,16,48]{0,2,1:T(8,128)(2,1)} %bitcast.67), kind=kOutput, calls=%fused_computation.64.clone.1 | convolution fusion | flops 105907200 | bytes 7966720 | tf_op jit(solution)/shard_map/while/body/eval_jaxpr/sub | solution.py:37
  299.8 3.5 fusion.70
  303.3 7.0 %select_add_fusion.2 = f32[16,64,1024]{2,1,0:T(8,128)} fusion(f32[16,64,1024]{2,1,0:T(8,128)} %get-tuple-element.193, bf16[64,16,48]{0,2,1:T(8,128)(2,1)S(1)} %bitcast.73, bf16[1024,16,48]{0,2,1:T(8,128)(2,1)} %bitcast.69, f32[16,64]{1,0:T(8,128)S(1)} %bitcast.82, pred[]{:T(512)S(6)} %compare.3, f32[16,64,1024]{2,1,0:T(8,128)} %get-tuple-element.179, ...), kind=kOutput, calls=%fused_computation.1.clone.1 | convolution fusion | flops 105906176 | bytes 14262273 | tf_op jit(solution)/shard_map/while/body/eval_jaxpr/ihe,jhe->hij/dot_general | solution.py:40
  310.4 0.7 constant_dynamic-update-slice_fusion.2
  311.0 1.0 constant_dynamic-slice_fusion.5
  312.2 3.8 constant_dynamic-slice_fusion.6
  315.9 4.7 %copy.59 = bf16[1,1024,1536]{1,2,0:T(8,128)(2,1)} copy(bf16[1,1024,1536]{2,1,0:T(8,128)(2,1)} %constant_dynamic-slice_fusion.6) | data formatting | bytes 6291456 | tf_op jit(solution)/shard_map/while/body/jit(dynamic_index_in_dim)/dynamic_slice | solution.py:90
  320.6 3.9 fusion.68
  324.5 5.7 %fusion.69 = (f32[16,64]{1,0:T(8,128)S(1)}, f32[16,64,1024]{2,1,0:T(8,128)}) fusion(bf16[16,64,1024]{2,1,0:T(8,128)(2,1)} %get-tuple-element.206, bf16[64,16,48]{0,2,1:T(8,128)(2,1)S(1)} %bitcast.70, bf16[1024,16,48]{0,2,1:T(8,128)(2,1)} %bitcast.67), kind=kOutput, calls=%fused_computation.64.clone.1 | convolution fusion | flops 105907200 | bytes 7966720 | tf_op jit(solution)/shard_map/while/body/eval_jaxpr/sub | solution.py:37
  330.4 3.5 fusion.70
  333.8 7.0 %select_add_fusion.2 = f32[16,64,1024]{2,1,0:T(8,128)} fusion(f32[16,64,1024]{2,1,0:T(8,128)} %get-tuple-element.193, bf16[64,16,48]{0,2,1:T(8,128)(2,1)S(1)} %bitcast.73, bf16[1024,16,48]{0,2,1:T(8,128)(2,1)} %bitcast.69, f32[16,64]{1,0:T(8,128)S(1)} %bitcast.82, pred[]{:T(512)S(6)} %compare.3, f32[16,64,1024]{2,1,0:T(8,128)} %get-tuple-element.179, ...), kind=kOutput, calls=%fused_computation.1.clone.1 | convolution fusion | flops 105906176 | bytes 14262273 | tf_op jit(solution)/shard_map/while/body/eval_jaxpr/ihe,jhe->hij/dot_general | solution.py:40
  340.9 0.7 constant_dynamic-update-slice_fusion.2
  341.6 1.0 constant_dynamic-slice_fusion.5
  342.7 3.8 constant_dynamic-slice_fusion.6
  346.5 4.7 %copy.59 = bf16[1,1024,1536]{1,2,0:T(8,128)(2,1)} copy(bf16[1,1024,1536]{2,1,0:T(8,128)(2,1)} %constant_dynamic-slice_fusion.6) | data formatting | bytes 6291456 | tf_op jit(solution)/shard_map/while/body/jit(dynamic_index_in_dim)/dynamic_slice | solution.py:90
  351.2 3.9 fusion.68
  355.1 5.7 %fusion.69 = (f32[16,64]{1,0:T(8,128)S(1)}, f32[16,64,1024]{2,1,0:T(8,128)}) fusion(bf16[16,64,1024]{2,1,0:T(8,128)(2,1)} %get-tuple-element.206, bf16[64,16,48]{0,2,1:T(8,128)(2,1)S(1)} %bitcast.70, bf16[1024,16,48]{0,2,1:T(8,128)(2,1)} %bitcast.67), kind=kOutput, calls=%fused_computation.64.clone.1 | convolution fusion | flops 105907200 | bytes 7966720 | tf_op jit(solution)/shard_map/while/body/eval_jaxpr/sub | solution.py:37
  360.9 3.5 fusion.70
  364.4 7.0 %select_add_fusion.2 = f32[16,64,1024]{2,1,0:T(8,128)} fusion(f32[16,64,1024]{2,1,0:T(8,128)} %get-tuple-element.193, bf16[64,16,48]{0,2,1:T(8,128)(2,1)S(1)} %bitcast.73, bf16[1024,16,48]{0,2,1:T(8,128)(2,1)} %bitcast.69, f32[16,64]{1,0:T(8,128)S(1)} %bitcast.82, pred[]{:T(512)S(6)} %compare.3, f32[16,64,1024]{2,1,0:T(8,128)} %get-tuple-element.179, ...), kind=kOutput, calls=%fused_computation.1.clone.1 | convolution fusion | flops 105906176 | bytes 14262273 | tf_op jit(solution)/shard_map/while/body/eval_jaxpr/ihe,jhe->hij/dot_general | solution.py:40
  371.5 0.7 constant_dynamic-update-slice_fusion.2
  372.2 2.2 fusion.43
  374.7 4.4 fusion.32
  379.1 2.3 fusion.23
  381.3 41.4 %reduce-scatter.2.cloned.1.call-done = f32[16,64,128]{2,1,0:T(8,128)} async-done(((f32[16,64,1024]{2,1,0:T(8,128)}), f32[16,64,128]{2,1,0:T(8,128)}) %reduce-scatter.2.cloned.1.call-update) | async-done | bytes 524304 | tf_op jit(solution)/shard_map/reduce_scatter | solution.py:92
  422.7 4.6 %fusion.40 = (f32[64,128]{1,0:T(8,128)S(1)}, f32[64,128]{1,0:T(8,128)S(1)}, f32[64,128,128]{1,2,0:T(8,128)S(1)}) fusion(f32[64,128]{1,0:T(8,128)S(1)} %add_rsqrt_fusion, f32[64,128]{1,0:T(8,128)S(1)} %broadcast_multiply_fusion.2, bf16[64,128,128]{1,2,0:T(8,128)(2,1)} %copy.27, bf16[128,16]{0,1:T(8,128)(2,1)S(1)} %copy-done.5, f32[64,128,16]{1,0,2:T(8,128)} %bitcast.79), kind=kOutput, calls=%fused_computation.62 | convolution fusion | flops 207601664 | bytes 6950912 | tf_op jit(solution)/shard_map/dot_general | solution.py:96
  427.4 3.2 fusion.17
  430.5 5.6 %copy.35 = f32[64,128,128]{2,1,0:T(8,128)} copy(f32[64,128,128]{1,2,0:T(8,128)} %fusion.17) | data formatting | bytes 8388608
  (50 shorter events, 4.5 us)
Async XLA Ops:
  7.2 371.9 %copy-start = (bf16[1536,768]{1,0:T(8,128)(2,1)S(1)}, bf16[1536,768]{1,0:T(8,128)(2,1)}, u32[]{:S(2)}) copy-start(bf16[1536,768]{1,0:T(8,128)(2,1)} %param.16) | copy-start | bytes 7077892
  7.2 54.3 %all-gather.5.cloned.1.call-start = ((), (), s32[]{:S(2)}) async-start(), calls=%async_computation.2 | async-start | bytes 2359296 | tf_op jit(solution)/shard_map/all_gather | solution.py:70
  11.4 2.3 copy-start.1
  11.4 3.1 copy-start.5
  13.7 3.5 copy-start.3
  17.2 172.8 %all-gather.3.cloned.1.call-start = ((), (), s32[]{:S(2)}) async-start(), calls=%async_computation.1 | async-start | bytes 20054016 | tf_op jit(solution)/shard_map/all_gather | solution.py:80
  17.9 4.0 copy-start.4
  21.9 400.8 %reduce-scatter.2.cloned.1.call-start = ((), (), s32[]{:S(2)}) async-start(), calls=%async_computation.3 | async-start | bytes 4718592 | tf_op jit(solution)/shard_map/reduce_scatter | solution.py:92
  422.7 4.6 %copy-start.2 = (bf16[64,128,128]{1,2,0:T(8,128)(2,1)S(1)}, bf16[64,128,128]{1,2,0:T(8,128)(2,1)}, u32[]{:S(2)}) copy-start(bf16[64,128,128]{1,2,0:T(8,128)(2,1)} %copy.27) | copy-start | bytes 6291460
Sparse Core Ops, SparseCore 0:
  17.3 44.1 all-gather.4
  64.0 125.9 all-gather.2
  372.3 50.3 reduce-scatter.1
where the time goes:
time: 444 us; the launch traced here: 443 us
  waiting for transfers between devices  202 us (45%)
  matrix products  118 us (27%)
  local copies, waits for them, and re-layouts  100 us (23%)
  between operations  13.9 us (3%)
  other arithmetic  7.22 us (2%)
    all_gather x1, waiting for transfers between devices, shards(): kv_all = lax.all_gather(kv_local, 'row', axis=1, tiled=True)  124 us
    dynamic_slice x30, local copies, waits for them, and re-layouts, shards(): lax.scan(one_sample, start_grad, (queries, kv_all, cotangent))  58.3 us
    reduce_scatter x1, waiting for transfers between devices, shards(): lax.psum_scatter(grad_local, 'col', scatter_dimension=2, tiled=True)  41.4 us
    dot_general x6, matrix products, attend_sample(): jnp.einsum('ihe,jhe->hij', cotan_h, value_h, preferred_element_type=jnp.f...  40.7 us
    all_gather x1, waiting for transfers between devices, shards(): lax.all_gather(project_pair(pair, bias_weight), 'col', axis=2, tiled=True)  36.6 us
    sub x6, matrix products, attend_sample(): weights = jax.nn.softmax(scores, axis=-1)  34.1 us
    slice x6, local copies, waits for them, and re-layouts, one_sample(): kv_s[:, :width]  23.5 us
    dot_general x6, matrix products, attend_sample(): jnp.einsum('hij,jhe->ihe', rounded, value_h, preferred_element_type=jnp.f...  20.8 us
  transfers between devices with their start and end apart: 3, of which 3 were waited for; matrix products, arithmetic and copies ran while one was open for 5% of the time, Pallas kernels for 0%

commit v1 on v0

--- a/solution.py
+++ b/solution.py
@@ -67,7 +67,11 @@
     width = single.shape[2]
     head_count = bias_weight.shape[1]
     samp_count, row_count = (single.shape[0], single.shape[1])
-    bias = lax.all_gather(project_pair(pair, bias_weight), "col", axis=2, tiled=True)
+    x = project_pair(pair, bias_weight)
+    count = lax.axis_size("col")
+    blocks = jnp.stack([x for _ in range(count)])
+    blocks = lax.all_to_all(blocks, "col", split_axis=0, concat_axis=0)
+    bias = jnp.concatenate(blocks, axis=2)
     normed = normalize(single.astype(jnp.float32))[0].astype(jnp.bfloat16)
     flat_normed = normed.reshape(samp_count * row_count, width)
     queries = jnp.dot(flat_normed, w_qkv[:, :width], preferred_element_type=jnp.float32).astype(

time: 444 us -> 412 us (0.928)
  waiting for transfers between devices: 202 us -> 163 us
  starting transfers between devices: 0.12 us -> 6.45 us
    all_gather x1 -> x0, waiting for transfers between devices: 36.6 us -> none  [shards(): lax.all_gather(project_pair(pair, bias_weight), 'col', axis=2, tiled=True)]
    all_gather x1, waiting for transfers between devices: 124 us -> 95 us  [shards(): kv_all = lax.all_gather(kv_local, 'row', axis=1, tiled=True)]
    all_to_all x0 -> x1, waiting for transfers between devices: none -> 27.8 us  [shards(): blocks = lax.all_to_all(blocks, 'col', split_axis=0, concat_axis=0)]
    all_to_all x0 -> x1, starting transfers between devices: none -> 6.37 us  [shards(): blocks = lax.all_to_all(blocks, 'col', split_axis=0, concat_axis=0)]
    unnamed x15 -> x20, local copies, waits for them, and re-layouts: 13.9 us -> 10.7 us
  transfers between devices with their start and end apart: 3 -> 3, of which waited for: 3 -> 3; matrix products, arithmetic and copies ran while one was open for 5% -> 6% of each run, Pallas kernels for 0% -> 0%
where the time goes in v1:
time: 412 us; the launch traced here: 411 us
  waiting for transfers between devices  163 us (40%)
  matrix products  117 us (28%)
  local copies, waits for them, and re-layouts  98.5 us (24%)
  between operations  14.3 us (3%)
  other arithmetic  10.6 us (3%)
  starting transfers between devices  6.45 us (2%)
    all_gather x1, waiting for transfers between devices, shards(): kv_all = lax.all_gather(kv_local, 'row', axis=1, tiled=True)  95 us
    dynamic_slice x30, local copies, waits for them, and re-layouts, shards(): lax.scan(one_sample, start_grad, (queries, kv_all, cotangent))  58.3 us
    dot_general x6, matrix products, attend_sample(): jnp.einsum('ihe,jhe->hij', cotan_h, value_h, preferred_element_type=jnp.f...  40.7 us
    reduce_scatter x1, waiting for transfers between devices, shards(): lax.psum_scatter(grad_local, 'col', scatter_dimension=2, tiled=True)  40.5 us
    sub x6, matrix products, attend_sample(): weights = jax.nn.softmax(scores, axis=-1)  34.1 us
    all_to_all x1, waiting for transfers between devices, shards(): blocks = lax.all_to_all(blocks, 'col', split_axis=0, concat_axis=0)  27.8 us
    slice x6, local copies, waits for them, and re-layouts, one_sample(): kv_s[:, :width]  23.5 us
    dot_general x6, matrix products, attend_sample(): jnp.einsum('hij,jhe->ihe', rounded, value_h, preferred_element_type=jnp.f...  20.8 us
  transfers between devices with their start and end apart: 3, of which 3 were waited for; matrix products, arithmetic and copies ran while one was open for 6% of the time, Pallas kernels for 0%

profile of v1, /device:TPU:1, one launch (start us, length us, event | category | flops | bytes accessed | tf_op | source)
XLA Modules:
  0.0 410.6 jit_solution(1937063838603152529)
XLA Ops:
  7.2 1.4 convert_reduce_fusion.1
  8.6 1.4 multiply_reduce_fusion.1
  10.0 1.3 multiply_convert_fusion.1
  11.3 3.8 convolution_convert_fusion
  15.1 4.1 copy.36
  19.1 2.2 convert_reduce_fusion
  22.3 1.8 fusion.29
  24.2 1.9 stack.2
  26.1 6.4 %all-to-all-start = ((bf16[8,16,64,128]{3,2,1,0:T(8,128)(2,1)}), bf16[8,16,64,128]{3,2,1,0:T(8,128)(2,1)}, u32[]{:S(2)}, u32[]{:S(2)}) async-start(bf16[8,16,64,128]{3,2,1,0:T(8,128)(2,1)} %stack.2), calls=%async_computation | async-start | bytes 4194304 | tf_op jit(solution)/shard_map/all_to_all | solution.py:73
  32.5 2.7 convolution_convert_fusion.1
  35.2 27.8 %all-to-all-done = bf16[8,16,64,128]{3,2,1,0:T(8,128)(2,1)} async-done(((bf16[8,16,64,128]{3,2,1,0:T(8,128)(2,1)}), bf16[8,16,64,128]{3,2,1,0:T(8,128)(2,1)}, u32[]{:S(2)}, u32[]{:S(2)}) %all-to-all-start) | async-done | bytes 2097184 | tf_op jit(solution)/shard_map/all_to_all | solution.py:73
  63.1 3.2 copy_bitcast_fusion
  66.3 95.0 %all-gather.2.cloned.1.call-done = bf16[6,1024,1536]{2,1,0:T(8,128)(2,1)} async-done(((bf16[6,64,1536]{2,1,0:T(8,128)(2,1)}), bf16[6,1024,1536]{2,1,0:T(8,128)(2,1)}) %all-gather.2.cloned.1.call-update) | async-done | bytes 18874384 | tf_op jit(solution)/shard_map/all_gather | solution.py:84
  161.3 178.5 %while.13 = (s32[]{:T(128)}, f32[16,64,1024]{2,1,0:T(8,128)}, bf16[6,64,768]{2,1,0:T(8,128)(2,1)S(1)}, bf16[6,64,768]{2,1,0:T(8,128)(2,1)}, bf16[6,1024,1536]{2,...) while((s32[]{:T(128)}, f32[16,64,1024]{2,1,0:T(8,128)}, ...), condition=%wide.region_8.9_spmd.clone, body=%wide.region_4.8_spmd.clone.sunk | while | flops 314769408 | bytes 48255088 | solution.py:94
  161.3 1.0 constant_dynamic-slice_fusion.5
  162.4 3.8 constant_dynamic-slice_fusion.6
  166.2 4.7 %copy.71 = bf16[1,1024,1536]{1,2,0:T(8,128)(2,1)} copy(bf16[1,1024,1536]{2,1,0:T(8,128)(2,1)} %constant_dynamic-slice_fusion.6) | data formatting | bytes 6291456 | tf_op jit(solution)/shard_map/while/body/jit(dynamic_index_in_dim)/dynamic_slice | solution.py:94
  170.9 3.9 fusion.69
  174.8 5.7 %fusion.70 = (f32[16,64]{1,0:T(8,128)S(1)}, f32[16,64,1024]{2,1,0:T(8,128)}) fusion(bf16[16,64,1024]{2,1,0:T(8,128)(2,1)} %get-tuple-element.215, bf16[64,16,48]{0,2,1:T(8,128)(2,1)S(1)} %bitcast.76, bf16[1024,16,48]{0,2,1:T(8,128)(2,1)} %bitcast.73), kind=kOutput, calls=%fused_computation.65.clone.1 | convolution fusion | flops 105907200 | bytes 7966720 | tf_op jit(solution)/shard_map/while/body/eval_jaxpr/sub | solution.py:37
  180.6 3.5 fusion.71
  184.1 5.8 %select_add_fusion.2 = f32[16,64,1024]{2,1,0:T(8,128)} fusion(f32[16,64,1024]{2,1,0:T(8,128)} %get-tuple-element.202, bf16[64,16,48]{0,2,1:T(8,128)(2,1)S(1)} %bitcast.79, bf16[1024,16,48]{0,2,1:T(8,128)(2,1)} %bitcast.75, f32[16,64]{1,0:T(8,128)S(1)} %bitcast.88, pred[]{:T(512)S(6)} %compare.3, f32[16,64,1024]{2,1,0:T(8,128)} %get-tuple-element.188, ...), kind=kOutput, calls=%fused_computation.1.clone.1 | convolution fusion | flops 105906176 | bytes 14262273 | tf_op jit(solution)/shard_map/while/body/eval_jaxpr/ihe,jhe->hij/dot_general | solution.py:40
  190.0 1.0 constant_dynamic-slice_fusion.5
  191.2 3.8 constant_dynamic-slice_fusion.6
  194.9 4.7 %copy.71 = bf16[1,1024,1536]{1,2,0:T(8,128)(2,1)} copy(bf16[1,1024,1536]{2,1,0:T(8,128)(2,1)} %constant_dynamic-slice_fusion.6) | data formatting | bytes 6291456 | tf_op jit(solution)/shard_map/while/body/jit(dynamic_index_in_dim)/dynamic_slice | solution.py:94
  199.6 3.9 fusion.69
  203.5 5.7 %fusion.70 = (f32[16,64]{1,0:T(8,128)S(1)}, f32[16,64,1024]{2,1,0:T(8,128)}) fusion(bf16[16,64,1024]{2,1,0:T(8,128)(2,1)} %get-tuple-element.215, bf16[64,16,48]{0,2,1:T(8,128)(2,1)S(1)} %bitcast.76, bf16[1024,16,48]{0,2,1:T(8,128)(2,1)} %bitcast.73), kind=kOutput, calls=%fused_computation.65.clone.1 | convolution fusion | flops 105907200 | bytes 7966720 | tf_op jit(solution)/shard_map/while/body/eval_jaxpr/sub | solution.py:37
  209.4 3.5 fusion.71
  212.8 7.0 %select_add_fusion.2 = f32[16,64,1024]{2,1,0:T(8,128)} fusion(f32[16,64,1024]{2,1,0:T(8,128)} %get-tuple-element.202, bf16[64,16,48]{0,2,1:T(8,128)(2,1)S(1)} %bitcast.79, bf16[1024,16,48]{0,2,1:T(8,128)(2,1)} %bitcast.75, f32[16,64]{1,0:T(8,128)S(1)} %bitcast.88, pred[]{:T(512)S(6)} %compare.3, f32[16,64,1024]{2,1,0:T(8,128)} %get-tuple-element.188, ...), kind=kOutput, calls=%fused_computation.1.clone.1 | convolution fusion | flops 105906176 | bytes 14262273 | tf_op jit(solution)/shard_map/while/body/eval_jaxpr/ihe,jhe->hij/dot_general | solution.py:40
  220.0 1.0 constant_dynamic-slice_fusion.5
  221.1 3.8 constant_dynamic-slice_fusion.6
  224.9 4.7 %copy.71 = bf16[1,1024,1536]{1,2,0:T(8,128)(2,1)} copy(bf16[1,1024,1536]{2,1,0:T(8,128)(2,1)} %constant_dynamic-slice_fusion.6) | data formatting | bytes 6291456 | tf_op jit(solution)/shard_map/while/body/jit(dynamic_index_in_dim)/dynamic_slice | solution.py:94
  229.6 3.9 fusion.69
  233.5 5.7 %fusion.70 = (f32[16,64]{1,0:T(8,128)S(1)}, f32[16,64,1024]{2,1,0:T(8,128)}) fusion(bf16[16,64,1024]{2,1,0:T(8,128)(2,1)} %get-tuple-element.215, bf16[64,16,48]{0,2,1:T(8,128)(2,1)S(1)} %bitcast.76, bf16[1024,16,48]{0,2,1:T(8,128)(2,1)} %bitcast.73), kind=kOutput, calls=%fused_computation.65.clone.1 | convolution fusion | flops 105907200 | bytes 7966720 | tf_op jit(solution)/shard_map/while/body/eval_jaxpr/sub | solution.py:37
  239.3 3.5 fusion.71
  242.8 7.0 %select_add_fusion.2 = f32[16,64,1024]{2,1,0:T(8,128)} fusion(f32[16,64,1024]{2,1,0:T(8,128)} %get-tuple-element.202, bf16[64,16,48]{0,2,1:T(8,128)(2,1)S(1)} %bitcast.79, bf16[1024,16,48]{0,2,1:T(8,128)(2,1)} %bitcast.75, f32[16,64]{1,0:T(8,128)S(1)} %bitcast.88, pred[]{:T(512)S(6)} %compare.3, f32[16,64,1024]{2,1,0:T(8,128)} %get-tuple-element.188, ...), kind=kOutput, calls=%fused_computation.1.clone.1 | convolution fusion | flops 105906176 | bytes 14262273 | tf_op jit(solution)/shard_map/while/body/eval_jaxpr/ihe,jhe->hij/dot_general | solution.py:40
  250.0 1.0 constant_dynamic-slice_fusion.5
  251.1 3.8 constant_dynamic-slice_fusion.6
  254.8 4.7 %copy.71 = bf16[1,1024,1536]{1,2,0:T(8,128)(2,1)} copy(bf16[1,1024,1536]{2,1,0:T(8,128)(2,1)} %constant_dynamic-slice_fusion.6) | data formatting | bytes 6291456 | tf_op jit(solution)/shard_map/while/body/jit(dynamic_index_in_dim)/dynamic_slice | solution.py:94
  259.5 3.9 fusion.69
  263.4 5.7 %fusion.70 = (f32[16,64]{1,0:T(8,128)S(1)}, f32[16,64,1024]{2,1,0:T(8,128)}) fusion(bf16[16,64,1024]{2,1,0:T(8,128)(2,1)} %get-tuple-element.215, bf16[64,16,48]{0,2,1:T(8,128)(2,1)S(1)} %bitcast.76, bf16[1024,16,48]{0,2,1:T(8,128)(2,1)} %bitcast.73), kind=kOutput, calls=%fused_computation.65.clone.1 | convolution fusion | flops 105907200 | bytes 7966720 | tf_op jit(solution)/shard_map/while/body/eval_jaxpr/sub | solution.py:37
  269.3 3.5 fusion.71
  272.8 7.0 %select_add_fusion.2 = f32[16,64,1024]{2,1,0:T(8,128)} fusion(f32[16,64,1024]{2,1,0:T(8,128)} %get-tuple-element.202, bf16[64,16,48]{0,2,1:T(8,128)(2,1)S(1)} %bitcast.79, bf16[1024,16,48]{0,2,1:T(8,128)(2,1)} %bitcast.75, f32[16,64]{1,0:T(8,128)S(1)} %bitcast.88, pred[]{:T(512)S(6)} %compare.3, f32[16,64,1024]{2,1,0:T(8,128)} %get-tuple-element.188, ...), kind=kOutput, calls=%fused_computation.1.clone.1 | convolution fusion | flops 105906176 | bytes 14262273 | tf_op jit(solution)/shard_map/while/body/eval_jaxpr/ihe,jhe->hij/dot_general | solution.py:40
  279.9 1.0 constant_dynamic-slice_fusion.5
  281.0 3.8 constant_dynamic-slice_fusion.6
  284.8 4.7 %copy.71 = bf16[1,1024,1536]{1,2,0:T(8,128)(2,1)} copy(bf16[1,1024,1536]{2,1,0:T(8,128)(2,1)} %constant_dynamic-slice_fusion.6) | data formatting | bytes 6291456 | tf_op jit(solution)/shard_map/while/body/jit(dynamic_index_in_dim)/dynamic_slice | solution.py:94
  289.5 3.9 fusion.69
  293.4 5.7 %fusion.70 = (f32[16,64]{1,0:T(8,128)S(1)}, f32[16,64,1024]{2,1,0:T(8,128)}) fusion(bf16[16,64,1024]{2,1,0:T(8,128)(2,1)} %get-tuple-element.215, bf16[64,16,48]{0,2,1:T(8,128)(2,1)S(1)} %bitcast.76, bf16[1024,16,48]{0,2,1:T(8,128)(2,1)} %bitcast.73), kind=kOutput, calls=%fused_computation.65.clone.1 | convolution fusion | flops 105907200 | bytes 7966720 | tf_op jit(solution)/shard_map/while/body/eval_jaxpr/sub | solution.py:37
  299.2 3.5 fusion.71
  302.7 7.0 %select_add_fusion.2 = f32[16,64,1024]{2,1,0:T(8,128)} fusion(f32[16,64,1024]{2,1,0:T(8,128)} %get-tuple-element.202, bf16[64,16,48]{0,2,1:T(8,128)(2,1)S(1)} %bitcast.79, bf16[1024,16,48]{0,2,1:T(8,128)(2,1)} %bitcast.75, f32[16,64]{1,0:T(8,128)S(1)} %bitcast.88, pred[]{:T(512)S(6)} %compare.3, f32[16,64,1024]{2,1,0:T(8,128)} %get-tuple-element.188, ...), kind=kOutput, calls=%fused_computation.1.clone.1 | convolution fusion | flops 105906176 | bytes 14262273 | tf_op jit(solution)/shard_map/while/body/eval_jaxpr/ihe,jhe->hij/dot_general | solution.py:40
  309.9 1.0 constant_dynamic-slice_fusion.5
  311.0 3.8 constant_dynamic-slice_fusion.6
  314.8 4.7 %copy.71 = bf16[1,1024,1536]{1,2,0:T(8,128)(2,1)} copy(bf16[1,1024,1536]{2,1,0:T(8,128)(2,1)} %constant_dynamic-slice_fusion.6) | data formatting | bytes 6291456 | tf_op jit(solution)/shard_map/while/body/jit(dynamic_index_in_dim)/dynamic_slice | solution.py:94
  319.4 3.9 fusion.69
  323.4 5.7 %fusion.70 = (f32[16,64]{1,0:T(8,128)S(1)}, f32[16,64,1024]{2,1,0:T(8,128)}) fusion(bf16[16,64,1024]{2,1,0:T(8,128)(2,1)} %get-tuple-element.215, bf16[64,16,48]{0,2,1:T(8,128)(2,1)S(1)} %bitcast.76, bf16[1024,16,48]{0,2,1:T(8,128)(2,1)} %bitcast.73), kind=kOutput, calls=%fused_computation.65.clone.1 | convolution fusion | flops 105907200 | bytes 7966720 | tf_op jit(solution)/shard_map/while/body/eval_jaxpr/sub | solution.py:37
  329.2 3.5 fusion.71
  332.7 7.0 %select_add_fusion.2 = f32[16,64,1024]{2,1,0:T(8,128)} fusion(f32[16,64,1024]{2,1,0:T(8,128)} %get-tuple-element.202, bf16[64,16,48]{0,2,1:T(8,128)(2,1)S(1)} %bitcast.79, bf16[1024,16,48]{0,2,1:T(8,128)(2,1)} %bitcast.75, f32[16,64]{1,0:T(8,128)S(1)} %bitcast.88, pred[]{:T(512)S(6)} %compare.3, f32[16,64,1024]{2,1,0:T(8,128)} %get-tuple-element.188, ...), kind=kOutput, calls=%fused_computation.1.clone.1 | convolution fusion | flops 105906176 | bytes 14262273 | tf_op jit(solution)/shard_map/while/body/eval_jaxpr/ihe,jhe->hij/dot_general | solution.py:40
  339.9 1.0 copy-done.3
  340.9 2.0 fusion.43
  343.2 4.4 %fusion.32 = f32[384,3072]{1,0:T(8,128)S(1)} fusion(bf16[768,3072]{1,0:T(8,128)(2,1)} %param.15, f32[384,768]{1,0:T(8,128)S(1)} %get-tuple-element.127, f32[384]{0:T(512)S(1)} %add_rsqrt_fusion.2, f32[384]{0:T(512)S(1)} %broadcast_multiply_fusion.4), kind=kOutput, calls=%fused_computation.47 | convolution fusion | flops 1812824064 | bytes 10619904 | tf_op jit(solution)/shard_map/dot_general | solution.py:53
  347.6 2.2 fusion.23
  349.8 40.5 %reduce-scatter.2.cloned.1.call-done = f32[16,64,128]{2,1,0:T(8,128)} async-done(((f32[16,64,1024]{2,1,0:T(8,128)}), f32[16,64,128]{2,1,0:T(8,128)}) %reduce-scatter.2.cloned.1.call-update) | async-done | bytes 524304 | tf_op jit(solution)/shard_map/reduce_scatter | solution.py:96
  390.4 4.6 %fusion.40 = (f32[64,128]{1,0:T(8,128)S(1)}, f32[64,128]{1,0:T(8,128)S(1)}, f32[64,128,128]{1,2,0:T(8,128)S(1)}) fusion(f32[64,128]{1,0:T(8,128)S(1)} %copy-done.7, f32[64,128]{1,0:T(8,128)S(1)} %copy-done.5, bf16[64,128,128]{1,2,0:T(8,128)(2,1)} %copy.36, bf16[128,16]{0,1:T(8,128)(2,1)S(1)} %copy-done.8, f32[64,128,16]{1,0,2:T(8,128)} %bitcast.85), kind=kOutput, calls=%fused_computation.63 | convolution fusion | flops 207601664 | bytes 6950912 | tf_op jit(solution)/shard_map/dot_general | solution.py:100
  395.0 3.2 fusion.17
  398.2 5.6 %copy.45 = f32[64,128,128]{2,1,0:T(8,128)} copy(f32[64,128,128]{1,2,0:T(8,128)} %fusion.17) | data formatting | bytes 8388608
  (57 shorter events, 4.2 us)
Async XLA Ops:
  7.2 340.4 %copy-start = (bf16[1536,768]{1,0:T(8,128)(2,1)S(1)}, bf16[1536,768]{1,0:T(8,128)(2,1)}, u32[]{:S(2)}) copy-start(bf16[1536,768]{1,0:T(8,128)(2,1)} %param.16) | copy-start | bytes 7077892
  7.2 154.1 %all-gather.2.cloned.1.call-start = ((), (), s32[]{:S(2)}) async-start(), calls=%async_computation.2 | async-start | bytes 20054016 | tf_op jit(solution)/shard_map/all_gather | solution.py:84
  19.1 2.3 copy-start.1
  19.1 3.1 copy-start.8
  21.4 2.7 copy-start.4
  22.3 1.8 copy-start.6
  26.1 37.0 %all-to-all-start = ((bf16[8,16,64,128]{3,2,1,0:T(8,128)(2,1)}), bf16[8,16,64,128]{3,2,1,0:T(8,128)(2,1)}, u32[]{:S(2)}, u32[]{:S(2)}) async-start(bf16[8,16,64,128]{3,2,1,0:T(8,128)(2,1)} %stack.2), calls=%async_computation | async-start | bytes 4194304 | tf_op jit(solution)/shard_map/all_to_all | solution.py:73
  32.5 357.9 %reduce-scatter.2.cloned.1.call-start = ((), (), s32[]{:S(2)}) async-start(), calls=%async_computation.3 | async-start | bytes 4718592 | tf_op jit(solution)/shard_map/reduce_scatter | solution.py:96
  339.8 1.1 copy-start.3
  347.6 42.8 %copy-start.5 = (f32[64,128]{1,0:T(8,128)S(1)}, f32[64,128]{1,0:T(8,128)}, u32[]{:S(2)}) copy-start(f32[64,128]{1,0:T(8,128)} %copy-done.4) | copy-start | bytes 98308
  347.6 42.8 %copy-start.7 = (f32[64,128]{1,0:T(8,128)S(1)}, f32[64,128]{1,0:T(8,128)}, u32[]{:S(2)}) copy-start(f32[64,128]{1,0:T(8,128)} %copy-done.6) | copy-start | bytes 98308
  390.4 4.7 %copy-start.2 = (bf16[64,128,128]{1,2,0:T(8,128)(2,1)S(1)}, bf16[64,128,128]{1,2,0:T(8,128)(2,1)}, u32[]{:S(2)}) copy-start(bf16[64,128,128]{1,2,0:T(8,128)(2,1)} %copy.36) | copy-start | bytes 6291460
Sparse Core Ops, SparseCore 0:
  15.2 146.0 all-gather.1
  340.0 50.3 reduce-scatter.1
